TPU v7x, 32 devices: a whole 2x2x4 slice. The times are simulated.
32 devices in a mesh: seq: 16 (over z, y, core), head: 2 (over x).
Axes of the slice: x: 2, y: 2, z: 4, core: 2. Of those that a mesh axis runs over, the one named last changes fastest.
Arguments:
- queries: bfloat16 [4, 64, 64, 128], P(None, None, 'head'), may hold values from -15 to 15
- new_keys: bfloat16 [4, 64, 8, 128], P(None, None, 'head'), may hold values from -16 to 16
- new_values: bfloat16 [4, 64, 8, 128], P(None, None, 'head'), may hold values from -6 to 6
- cache_keys: bfloat16 [4, 32768, 8, 128], P(None, 'seq', 'head'), may hold values from -6 to 6
- cache_values: bfloat16 [4, 32768, 8, 128], P(None, 'seq', 'head'), may hold values from -6 to 6
- parents: int32 [4, 64], replicated, may hold values from 0 to 63, as said below
- kv_lengths: int32 [4], replicated, may hold values from 1 to 32768
- out_weight: bfloat16 [8192, 8192], P('head', 'seq'), may hold values from -0.5 to 0.5
Outputs:
- mixed: bfloat16 [256, 8192], P('head', 'seq')
Inputs may be any that keep to these rules, and one draw needn't show every extreme that they name: parents[r, 0] = 0 for the root; for i >= 1, parents[r, i] < i.
All inputs are finite; a program needn't handle non-finite values.
Results may differ from a plain program's by a relative error of at most 0.0045.
Values may be sent and summed in bfloat16 or wider, within the bound.
A program may use at most 128 MiB of HBM per device.

v0:
```python
import math
import jax
import jax.numpy as jnp
from jax import lax
from jax.sharding import PartitionSpec as P

lowest = -1e30


def ancestors(parent_row):
    tree_size = parent_row.shape[0]
    indices = jnp.arange(tree_size, dtype=jnp.int32)
    parent_link = (parent_row[:, None] == indices[None, :]).astype(jnp.float32)
    itself = (indices[:, None] == indices[None, :]).astype(jnp.float32)
    reached = jnp.maximum(parent_link, itself)
    for repeat in range(max(1, (tree_size - 1).bit_length())):
        reached = jnp.minimum(jnp.dot(reached, reached, precision=lax.Precision.HIGHEST), 1.0)
    return reached


def partial_scores(query_rows, keys, values, allowed, score_scale):
    scores = (
        jnp.einsum("kqd,pkd->kqp", query_rows, keys, preferred_element_type=jnp.float32)
        * score_scale
    )
    scores = jnp.where(allowed, scores, lowest)
    maxima = jnp.max(scores, axis=-1)
    weights = jnp.where(allowed, jnp.exp(scores - maxima[..., None]), 0.0)
    totals = jnp.sum(weights, axis=-1)
    weighted = jnp.einsum(
        "kqp,pkd->kqd", weights.astype(jnp.bfloat16), values, preferred_element_type=jnp.float32
    )
    return (maxima, totals, weighted)


def body(queries, new_keys, new_values, cache_keys, cache_values, parents, kv_lengths, out_weight):
    requests, tree_size, heads, head_size = queries.shape
    kv_heads = new_keys.shape[2]
    group_size = heads // kv_heads
    block_size = cache_keys.shape[1]
    score_scale = 1.0 / math.sqrt(head_size)
    tokens = requests * tree_size
    positions = lax.axis_index("seq") * block_size + jnp.arange(block_size, dtype=jnp.int32)

    def token_order(maxima, totals, weighted):
        maxima = (
            maxima.reshape(kv_heads, tree_size, group_size)
            .transpose(1, 0, 2)
            .reshape(tree_size, heads)
        )
        totals = (
            totals.reshape(kv_heads, tree_size, group_size)
            .transpose(1, 0, 2)
            .reshape(tree_size, heads)
        )
        weighted = weighted.reshape(kv_heads, tree_size, group_size, head_size).transpose(
            1, 0, 2, 3
        )
        return (maxima, totals, weighted.reshape(tree_size, heads, head_size))

    def one_request(request_items):
        query, tree_keys, tree_values, past_keys, past_values, parent_row, length = request_items
        query_rows = query.reshape(tree_size, kv_heads, group_size, head_size).transpose(1, 0, 2, 3)
        query_rows = query_rows.reshape(kv_heads, tree_size * group_size, head_size)
        cache_max, cache_tot, cache_acc = partial_scores(
            query_rows, past_keys, past_values, positions < length, score_scale
        )
        tree_allowed = jnp.repeat(ancestors(parent_row), group_size, axis=0) > 0.5
        tree_max, tree_tot, tree_acc = partial_scores(
            query_rows, tree_keys, tree_values, tree_allowed, score_scale
        )
        return (
            token_order(cache_max, cache_tot, cache_acc),
            token_order(tree_max, tree_tot, tree_acc),
        )

    cache_part, tree_part = lax.map(
        one_request, (queries, new_keys, new_values, cache_keys, cache_values, parents, kv_lengths)
    )
    cache_max = cache_part[0].reshape(tokens, heads)
    cache_tot = cache_part[1].reshape(tokens, heads)
    cache_acc = cache_part[2].reshape(tokens, heads, head_size)
    tree_max = tree_part[0].reshape(tokens, heads)
    tree_tot = tree_part[1].reshape(tokens, heads)
    tree_acc = tree_part[2].reshape(tokens, heads, head_size)
    overall = lax.pmax(cache_max, "seq")
    overall = jnp.maximum(overall, tree_max)
    factor = jnp.exp(cache_max - overall)
    shared_acc, shared_tot = (
        lax.psum_scatter(cache_acc * factor[..., None], "seq", scatter_dimension=0, tiled=True),
        lax.psum_scatter(cache_tot * factor, "seq", scatter_dimension=0, tiled=True),
    )
    row_count = tokens // lax.axis_size("seq")
    first_row = lax.axis_index("seq") * row_count

    def take_rows(array):
        return lax.dynamic_slice_in_dim(array, first_row, row_count, 0)

    tree_factor = jnp.exp(take_rows(tree_max) - take_rows(overall))
    weighted = shared_acc + take_rows(tree_acc) * tree_factor[..., None]
    totals = shared_tot + take_rows(tree_tot) * tree_factor
    share = (
        (weighted / totals[..., None]).astype(jnp.bfloat16).reshape(row_count, heads * head_size)
    )
    attended = lax.all_gather(share, "seq", axis=0, tiled=True)
    mixed = lax.psum_scatter(
        jnp.dot(attended, out_weight, preferred_element_type=jnp.float32),
        "head",
        scatter_dimension=0,
        tiled=True,
    )
    return mixed.astype(jnp.bfloat16)


def solution(mesh):
    placed = (
        P(None, None, "head", None),
        P(None, None, "head", None),
        P(None, None, "head", None),
        P(None, "seq", "head", None),
        P(None, "seq", "head", None),
        P(),
        P(),
        P("head", "seq"),
    )
    return jax.shard_map(
        body, mesh=mesh, in_specs=placed, out_specs=P("head", "seq"), check_vma=False
    )
```

profile of v0, /device:TPU:0, one launch (start us, length us, event | category | flops | bytes accessed | tf_op | source)
XLA Modules:
  0.0 414.5 jit_solution(2779970047454667348)
XLA Ops:
  6.5 145.8 %while.21 = (s32[]{:T(128)}, f32[4,64,32]{1,0,2:T(4,128)S(1)}, f32[4,64,32]{1,0,2:T(4,128)S(1)}, f32[4,64,32,128]{3,2,1,0:T(8,128)}, f32[4,64,32]{1,0,2:T(4,128)...) while((s32[]{:T(128)}, f32[4,64,32]{1,0,2:T(4,128)S(1)}, ...), condition=%wide.region_5.6_spmd.clone, body=%wide.region_0.5_spmd.clone.sunk | while | flops 2289217536 | bytes 81249280 | solution.py:77
  8.7 2.0 constant_dynamic-slice_fusion.9
  10.7 7.2 %fusion.81 = (f32[4,512]{1,0:T(4,128)S(1)}, f32[4,512,2048]{2,1,0:T(8,128)}) fusion(pred[2048]{0:T(1024)(128)(4,1)S(1)} %add_compare_fusion.2, bf16[1,2048,4,128]{3,2,1,0:T(4,128)(2,1)S(1)} %constant_dynamic-slice_fusion.9, bf16[4,64,32,128]{3,2,1,0:T(8,128)(2,1)S(1)} %copy-done, s32[]{:T(128)S(6)} %copy.150), kind=kOutput, calls=%fused_computation.3.clone.1 | convolution fusion | flops 1086322688 | bytes 19408900 | tf_op jit(solution)/shard_map/while/body/eval_jaxpr/kqd,pkd->kqp/dot_general | solution.py:23
  18.2 8.1 %fusion.82 = f32[4,512]{1,0:T(4,128)S(1)} fusion(f32[4,512,2048]{2,1,0:T(8,128)} %get-tuple-element.325, f32[4,512]{1,0:T(4,128)S(1)} %get-tuple-element.324, pred[2048]{0:T(1024)(128)(4,1)S(1)} %add_compare_fusion.2), kind=kLoop, calls=%fused_computation.5.clone.1 | loop fusion | flops 20969472 | bytes 16795648 | tf_op jit(solution)/shard_map/while/body/eval_jaxpr/reduce_sum | solution.py:29
  31.0 2.0 constant_dynamic-slice_fusion.12
  33.0 7.7 %fusion.86 = f32[64,4,8,128]{3,2,0,1:T(8,128)S(1)} fusion(bf16[1,2048,4,128]{3,2,1,0:T(4,128)(2,1)S(1)} %constant_dynamic-slice_fusion.12, f32[4,512,2048]{2,1,0:T(8,128)} %get-tuple-element.325, f32[4,512]{1,0:T(4,128)S(1)} %get-tuple-element.324, pred[2048]{0:T(1024)(128)(4,1)S(1)} %add_compare_fusion.2), kind=kOutput, calls=%fused_computation.11.clone.1 | convolution fusion | flops 1094713344 | bytes 19933184 | tf_op jit(solution)/shard_map/while/body/eval_jaxpr/kqp,pkd->kqd/dot_general | solution.py:30
  45.2 2.0 constant_dynamic-slice_fusion.9
  47.2 7.2 %fusion.81 = (f32[4,512]{1,0:T(4,128)S(1)}, f32[4,512,2048]{2,1,0:T(8,128)}) fusion(pred[2048]{0:T(1024)(128)(4,1)S(1)} %add_compare_fusion.2, bf16[1,2048,4,128]{3,2,1,0:T(4,128)(2,1)S(1)} %constant_dynamic-slice_fusion.9, bf16[4,64,32,128]{3,2,1,0:T(8,128)(2,1)S(1)} %copy-done, s32[]{:T(128)S(6)} %copy.150), kind=kOutput, calls=%fused_computation.3.clone.1 | convolution fusion | flops 1086322688 | bytes 19408900 | tf_op jit(solution)/shard_map/while/body/eval_jaxpr/kqd,pkd->kqp/dot_general | solution.py:23
  54.7 8.1 %fusion.82 = f32[4,512]{1,0:T(4,128)S(1)} fusion(f32[4,512,2048]{2,1,0:T(8,128)} %get-tuple-element.325, f32[4,512]{1,0:T(4,128)S(1)} %get-tuple-element.324, pred[2048]{0:T(1024)(128)(4,1)S(1)} %add_compare_fusion.2), kind=kLoop, calls=%fused_computation.5.clone.1 | loop fusion | flops 20969472 | bytes 16795648 | tf_op jit(solution)/shard_map/while/body/eval_jaxpr/reduce_sum | solution.py:29
  67.5 2.0 constant_dynamic-slice_fusion.12
  69.5 7.7 %fusion.86 = f32[64,4,8,128]{3,2,0,1:T(8,128)S(1)} fusion(bf16[1,2048,4,128]{3,2,1,0:T(4,128)(2,1)S(1)} %constant_dynamic-slice_fusion.12, f32[4,512,2048]{2,1,0:T(8,128)} %get-tuple-element.325, f32[4,512]{1,0:T(4,128)S(1)} %get-tuple-element.324, pred[2048]{0:T(1024)(128)(4,1)S(1)} %add_compare_fusion.2), kind=kOutput, calls=%fused_computation.11.clone.1 | convolution fusion | flops 1094713344 | bytes 19933184 | tf_op jit(solution)/shard_map/while/body/eval_jaxpr/kqp,pkd->kqd/dot_general | solution.py:30
  83.7 7.2 %fusion.81 = (f32[4,512]{1,0:T(4,128)S(1)}, f32[4,512,2048]{2,1,0:T(8,128)}) fusion(pred[2048]{0:T(1024)(128)(4,1)S(1)} %add_compare_fusion.2, bf16[1,2048,4,128]{3,2,1,0:T(4,128)(2,1)S(1)} %constant_dynamic-slice_fusion.9, bf16[4,64,32,128]{3,2,1,0:T(8,128)(2,1)S(1)} %copy-done, s32[]{:T(128)S(6)} %copy.150), kind=kOutput, calls=%fused_computation.3.clone.1 | convolution fusion | flops 1086322688 | bytes 19408900 | tf_op jit(solution)/shard_map/while/body/eval_jaxpr/kqd,pkd->kqp/dot_general | solution.py:23
  91.2 8.1 %fusion.82 = f32[4,512]{1,0:T(4,128)S(1)} fusion(f32[4,512,2048]{2,1,0:T(8,128)} %get-tuple-element.325, f32[4,512]{1,0:T(4,128)S(1)} %get-tuple-element.324, pred[2048]{0:T(1024)(128)(4,1)S(1)} %add_compare_fusion.2), kind=kLoop, calls=%fused_computation.5.clone.1 | loop fusion | flops 20969472 | bytes 16795648 | tf_op jit(solution)/shard_map/while/body/eval_jaxpr/reduce_sum | solution.py:29
  105.9 7.7 %fusion.86 = f32[64,4,8,128]{3,2,0,1:T(8,128)S(1)} fusion(bf16[1,2048,4,128]{3,2,1,0:T(4,128)(2,1)S(1)} %constant_dynamic-slice_fusion.12, f32[4,512,2048]{2,1,0:T(8,128)} %get-tuple-element.325, f32[4,512]{1,0:T(4,128)S(1)} %get-tuple-element.324, pred[2048]{0:T(1024)(128)(4,1)S(1)} %add_compare_fusion.2), kind=kOutput, calls=%fused_computation.11.clone.1 | convolution fusion | flops 1094713344 | bytes 19933184 | tf_op jit(solution)/shard_map/while/body/eval_jaxpr/kqp,pkd->kqd/dot_general | solution.py:30
  120.1 7.2 %fusion.81 = (f32[4,512]{1,0:T(4,128)S(1)}, f32[4,512,2048]{2,1,0:T(8,128)}) fusion(pred[2048]{0:T(1024)(128)(4,1)S(1)} %add_compare_fusion.2, bf16[1,2048,4,128]{3,2,1,0:T(4,128)(2,1)S(1)} %constant_dynamic-slice_fusion.9, bf16[4,64,32,128]{3,2,1,0:T(8,128)(2,1)S(1)} %copy-done, s32[]{:T(128)S(6)} %copy.150), kind=kOutput, calls=%fused_computation.3.clone.1 | convolution fusion | flops 1086322688 | bytes 19408900 | tf_op jit(solution)/shard_map/while/body/eval_jaxpr/kqd,pkd->kqp/dot_general | solution.py:23
  127.6 8.1 %fusion.82 = f32[4,512]{1,0:T(4,128)S(1)} fusion(f32[4,512,2048]{2,1,0:T(8,128)} %get-tuple-element.325, f32[4,512]{1,0:T(4,128)S(1)} %get-tuple-element.324, pred[2048]{0:T(1024)(128)(4,1)S(1)} %add_compare_fusion.2), kind=kLoop, calls=%fused_computation.5.clone.1 | loop fusion | flops 20969472 | bytes 16795648 | tf_op jit(solution)/shard_map/while/body/eval_jaxpr/reduce_sum | solution.py:29
  142.4 7.7 %fusion.86 = f32[64,4,8,128]{3,2,0,1:T(8,128)S(1)} fusion(bf16[1,2048,4,128]{3,2,1,0:T(4,128)(2,1)S(1)} %constant_dynamic-slice_fusion.12, f32[4,512,2048]{2,1,0:T(8,128)} %get-tuple-element.325, f32[4,512]{1,0:T(4,128)S(1)} %get-tuple-element.324, pred[2048]{0:T(1024)(128)(4,1)S(1)} %add_compare_fusion.2), kind=kOutput, calls=%fused_computation.11.clone.1 | convolution fusion | flops 1094713344 | bytes 19933184 | tf_op jit(solution)/shard_map/while/body/eval_jaxpr/kqp,pkd->kqd/dot_general | solution.py:30
  152.6 63.0 %pmax.7 = f32[256,32]{0,1:T(8,128)S(1)} all-reduce(f32[256,32]{0,1:T(8,128)S(1)} %reshape.69), channel_id=1, replica_groups=mesh['seq'=16,'head'=2] {'seq'}, use_global_device_ids=true, to_apply=%region_6.7 | all-reduce | flops 8192 | bytes 65536 | tf_op jit(solution)/shard_map/pmax | solution.py:86
  216.6 4.1 %bitcast_multiply_fusion = f32[256,32,128]{2,1,0:T(8,128)} fusion(f32[4,64,32,128]{3,2,1,0:T(8,128)} %get-tuple-element.87, f32[256,32]{1,0:T(8,128)S(1)} %copy.63), kind=kLoop, calls=%fused_computation.55 | loop fusion | flops 1048576 | bytes 8421376 | tf_op jit(solution)/shard_map/mul | solution.py:90
  221.0 48.6 %reduce-scatter.10.cloned.1.call-done = f32[16,32]{1,0:T(8,128)} async-done(((f32[256,32]{1,0:T(8,128)}), f32[16,32]{1,0:T(8,128)}) %reduce-scatter.10.cloned.1.call-update) | async-done | bytes 2064
  270.5 74.7 %reduce-scatter.6.cloned.1.call-done = f32[16,32,128]{2,1,0:T(8,128)} async-done(((f32[256,32,128]{2,1,0:T(8,128)}), f32[16,32,128]{2,1,0:T(8,128)}) %reduce-scatter.6.cloned.1.call-update) | async-done | bytes 262160 | tf_op jit(solution)/shard_map/reduce_scatter | solution.py:90
  347.2 40.7 %all-gather.2.cloned.1.call-done = bf16[256,4096]{1,0:T(8,128)(2,1)} async-done(((bf16[16,4096]{1,0:T(8,128)(2,1)}), bf16[256,4096]{1,0:T(8,128)(2,1)}) %all-gather.2.cloned.1.call-update) | async-done | bytes 2097168 | tf_op jit(solution)/shard_map/all_gather | solution.py:105
  387.9 4.9 %fusion.35 = f32[256,512]{1,0:T(8,128)} fusion(bf16[256,4096]{1,0:T(8,128)(2,1)} %all-gather.2.cloned.1.call-done, bf16[4096,512]{1,0:T(8,128)(2,1)} %param.17), kind=kOutput, calls=%fused_computation.63 | convolution fusion | flops 1073741824 | bytes 6815744 | tf_op jit(solution)/shard_map/dot_general | solution.py:107
  392.8 13.5 %reduce-scatter.8.cloned.1.call-done = f32[128,512]{1,0:T(8,128)} async-done(((f32[256,512]{1,0:T(8,128)}), f32[128,512]{1,0:T(8,128)}) %reduce-scatter.8.cloned.1.call-update) | async-done | bytes 262160 | tf_op jit(solution)/shard_map/reduce_scatter | solution.py:106
  (156 shorter events, 51.4 us)
Async XLA Ops:
  6.5 263.0 %reduce-scatter.10.cloned.1.call-start = ((), (), s32[]{:S(2)}) async-start(), calls=%async_computation.6 | async-start | bytes 139264
  6.6 4.2 %copy-start = (bf16[4,64,32,128]{3,2,1,0:T(8,128)(2,1)S(1)}, bf16[4,64,32,128]{3,2,1,0:T(8,128)(2,1)}, u32[]{:S(2)}) copy-start(bf16[4,64,32,128]{3,2,1,0:T(8,128)(2,1)} %get-tuple-element.372) | copy-start | bytes 6291460 | tf_op jit(solution)/shard_map/while
  43.0 4.2 %copy-start = (bf16[4,64,32,128]{3,2,1,0:T(8,128)(2,1)S(1)}, bf16[4,64,32,128]{3,2,1,0:T(8,128)(2,1)}, u32[]{:S(2)}) copy-start(bf16[4,64,32,128]{3,2,1,0:T(8,128)(2,1)} %get-tuple-element.372) | copy-start | bytes 6291460 | tf_op jit(solution)/shard_map/while
  79.5 4.2 %copy-start = (bf16[4,64,32,128]{3,2,1,0:T(8,128)(2,1)S(1)}, bf16[4,64,32,128]{3,2,1,0:T(8,128)(2,1)}, u32[]{:S(2)}) copy-start(bf16[4,64,32,128]{3,2,1,0:T(8,128)(2,1)} %get-tuple-element.372) | copy-start | bytes 6291460 | tf_op jit(solution)/shard_map/while
  116.0 4.2 %copy-start = (bf16[4,64,32,128]{3,2,1,0:T(8,128)(2,1)S(1)}, bf16[4,64,32,128]{3,2,1,0:T(8,128)(2,1)}, u32[]{:S(2)}) copy-start(bf16[4,64,32,128]{3,2,1,0:T(8,128)(2,1)} %get-tuple-element.372) | copy-start | bytes 6291460 | tf_op jit(solution)/shard_map/while
  216.5 128.7 %reduce-scatter.6.cloned.1.call-start = ((), (), s32[]{:S(2)}) async-start(), calls=%async_computation.3 | async-start | bytes 4456448 | tf_op jit(solution)/shard_map/reduce_scatter | solution.py:90
  220.8 167.1 %all-gather.2.cloned.1.call-start = ((), (), s32[]{:S(2)}) async-start(), calls=%async_computation.4 | async-start | bytes 2228224 | tf_op jit(solution)/shard_map/all_gather | solution.py:105
  347.2 59.1 %reduce-scatter.8.cloned.1.call-start = ((), (), s32[]{:S(2)}) async-start(), calls=%async_computation.5 | async-start | bytes 786432 | tf_op jit(solution)/shard_map/reduce_scatter | solution.py:106
Sparse Core Ops, SparseCore 0:
  216.6 52.8 reduce-scatter.9
  273.4 71.7 reduce-scatter.5
  347.4 40.4 all-gather.1
  392.9 13.3 reduce-scatter.7
where the time goes:
time: 416 us; the launch traced here: 414 us
  waiting for transfers between devices  178 us (43%)
  matrix products  71.1 us (17%)
  blocking collectives  63 us (15%)
  local copies, waits for them, and re-layouts  46 us (11%)
  other arithmetic  42.7 us (10%)
  between operations  13.2 us (3%)
    reduce_scatter x1, waiting for transfers between devices, body(): lax.psum_scatter(cache_acc * factor[..., None], 'seq', scatter_dimension=...  74.7 us
    pmax x1, blocking collectives, body(): overall = lax.pmax(cache_max, 'seq')  63 us
    unnamed x5, waiting for transfers between devices  48.6 us
    all_gather x1, waiting for transfers between devices, body(): attended = lax.all_gather(share, 'seq', axis=0, tiled=True)  40.7 us
    reduce_sum x8, other arithmetic, partial_scores(): totals = jnp.sum(weights, axis=-1)  32.9 us
    dot_general x8, matrix products, partial_scores(): jnp.einsum('kqp,pkd->kqd', weights.astype(jnp.bfloat16), values, preferre...  32.1 us
    dot_general x8, matrix products, partial_scores(): jnp.einsum('kqd,pkd->kqp', query_rows, keys, preferred_element_type=jnp.f...  30 us
    dynamic_slice x20, local copies, waits for them, and re-layouts, body(): lax.map(one_request, (queries, new_keys, new_values, cache_keys, cache_va...  28.8 us
  transfers between devices with their start and end apart: 4, of which 4 were waited for; matrix products, arithmetic and copies ran while one was open for 1% of the time, Pallas kernels for 0%

commit v1 on v0

--- a/solution.py
+++ b/solution.py
@@ -102,7 +102,9 @@
     share = (
         (weighted / totals[..., None]).astype(jnp.bfloat16).reshape(row_count, heads * head_size)
     )
-    attended = lax.all_gather(share, "seq", axis=0, tiled=True)
+    attended = jnp.concatenate(
+        lax.all_to_all(jnp.stack([share] * lax.axis_size("seq")), "seq", 0, 0), axis=0
+    )
     mixed = lax.psum_scatter(
         jnp.dot(attended, out_weight, preferred_element_type=jnp.float32),
         "head",

time: 416 us -> 424 us (1.019)
  blocking collectives: 63 us -> 114 us
  waiting for transfers between devices: 178 us -> 139 us
    all_to_all x0 -> x1, blocking collectives: none -> 50.7 us  [body(): lax.all_to_all(jnp.stack([share] * lax.axis_size('seq')), 'seq', 0, 0)]
    all_gather x1 -> x0, waiting for transfers between devices: 40.7 us -> none  [body(): attended = lax.all_gather(share, 'seq', axis=0, tiled=True)]
    unnamed x5 -> x4, waiting for transfers between devices: 48.6 us -> 48.6 us
  transfers between devices with their start and end apart: 4 -> 3, of which waited for: 4 -> 3; matrix products, arithmetic and copies ran while one was open for 1% -> 1% of each run, Pallas kernels for 0% -> 0%
where the time goes in v1:
time: 424 us; the launch traced here: 423 us
  waiting for transfers between devices  139 us (33%)
  blocking collectives  114 us (27%)
  matrix products  68.3 us (16%)
  local copies, waits for them, and re-layouts  45.6 us (11%)
  other arithmetic  42.9 us (10%)
  between operations  13.2 us (3%)
    reduce_scatter x1, waiting for transfers between devices, body(): lax.psum_scatter(cache_acc * factor[..., None], 'seq', scatter_dimension=...  74.7 us
    pmax x1, blocking collectives, body(): overall = lax.pmax(cache_max, 'seq')  63 us
    all_to_all x1, blocking collectives, body(): lax.all_to_all(jnp.stack([share] * lax.axis_size('seq')), 'seq', 0, 0)  50.7 us
    unnamed x4, waiting for transfers between devices  48.6 us
    reduce_sum x8, other arithmetic, partial_scores(): totals = jnp.sum(weights, axis=-1)  32.9 us
    dot_general x8, matrix products, partial_scores(): jnp.einsum('kqp,pkd->kqd', weights.astype(jnp.bfloat16), values, preferre...  32.1 us
    dot_general x8, matrix products, partial_scores(): jnp.einsum('kqd,pkd->kqp', query_rows, keys, preferred_element_type=jnp.f...  30 us
    dynamic_slice x20, local copies, waits for them, and re-layouts, body(): lax.map(one_request, (queries, new_keys, new_values, cache_keys, cache_va...  28.8 us
  transfers between devices with their start and end apart: 3, of which 3 were waited for; matrix products, arithmetic and copies ran while one was open for 1% of the time, Pallas kernels for 0%

profile of v1, /device:TPU:0, one launch (start us, length us, event | category | flops | bytes accessed | tf_op | source)
XLA Modules:
  0.0 423.1 jit_solution(15765110066268389310)
XLA Ops:
  6.5 145.8 %while.21 = (s32[]{:T(128)}, f32[4,64,32]{1,0,2:T(4,128)S(1)}, f32[4,64,32]{1,0,2:T(4,128)S(1)}, f32[4,64,32,128]{3,2,1,0:T(8,128)}, f32[4,64,32]{1,0,2:T(4,128)...) while((s32[]{:T(128)}, f32[4,64,32]{1,0,2:T(4,128)S(1)}, ...), condition=%wide.region_5.6_spmd.clone, body=%wide.region_0.5_spmd.clone.sunk | while | flops 2289217536 | bytes 81249280 | solution.py:77
  8.7 2.0 constant_dynamic-slice_fusion.9
  10.7 7.2 %fusion.81 = (f32[4,512]{1,0:T(4,128)S(1)}, f32[4,512,2048]{2,1,0:T(8,128)}) fusion(pred[2048]{0:T(1024)(128)(4,1)S(1)} %add_compare_fusion.2, bf16[1,2048,4,128]{3,2,1,0:T(4,128)(2,1)S(1)} %constant_dynamic-slice_fusion.9, bf16[4,64,32,128]{3,2,1,0:T(8,128)(2,1)S(1)} %copy-done, s32[]{:T(128)S(6)} %copy.150), kind=kOutput, calls=%fused_computation.3.clone.1 | convolution fusion | flops 1086322688 | bytes 19408900 | tf_op jit(solution)/shard_map/while/body/eval_jaxpr/kqd,pkd->kqp/dot_general | solution.py:23
  18.2 8.1 %fusion.82 = f32[4,512]{1,0:T(4,128)S(1)} fusion(f32[4,512,2048]{2,1,0:T(8,128)} %get-tuple-element.325, f32[4,512]{1,0:T(4,128)S(1)} %get-tuple-element.324, pred[2048]{0:T(1024)(128)(4,1)S(1)} %add_compare_fusion.2), kind=kLoop, calls=%fused_computation.5.clone.1 | loop fusion | flops 20969472 | bytes 16795648 | tf_op jit(solution)/shard_map/while/body/eval_jaxpr/reduce_sum | solution.py:29
  31.0 2.0 constant_dynamic-slice_fusion.12
  33.0 7.7 %fusion.86 = f32[64,4,8,128]{3,2,0,1:T(8,128)S(1)} fusion(bf16[1,2048,4,128]{3,2,1,0:T(4,128)(2,1)S(1)} %constant_dynamic-slice_fusion.12, f32[4,512,2048]{2,1,0:T(8,128)} %get-tuple-element.325, f32[4,512]{1,0:T(4,128)S(1)} %get-tuple-element.324, pred[2048]{0:T(1024)(128)(4,1)S(1)} %add_compare_fusion.2), kind=kOutput, calls=%fused_computation.11.clone.1 | convolution fusion | flops 1094713344 | bytes 19933184 | tf_op jit(solution)/shard_map/while/body/eval_jaxpr/kqp,pkd->kqd/dot_general | solution.py:30
  45.2 2.0 constant_dynamic-slice_fusion.9
  47.2 7.2 %fusion.81 = (f32[4,512]{1,0:T(4,128)S(1)}, f32[4,512,2048]{2,1,0:T(8,128)}) fusion(pred[2048]{0:T(1024)(128)(4,1)S(1)} %add_compare_fusion.2, bf16[1,2048,4,128]{3,2,1,0:T(4,128)(2,1)S(1)} %constant_dynamic-slice_fusion.9, bf16[4,64,32,128]{3,2,1,0:T(8,128)(2,1)S(1)} %copy-done, s32[]{:T(128)S(6)} %copy.150), kind=kOutput, calls=%fused_computation.3.clone.1 | convolution fusion | flops 1086322688 | bytes 19408900 | tf_op jit(solution)/shard_map/while/body/eval_jaxpr/kqd,pkd->kqp/dot_general | solution.py:23
  54.7 8.1 %fusion.82 = f32[4,512]{1,0:T(4,128)S(1)} fusion(f32[4,512,2048]{2,1,0:T(8,128)} %get-tuple-element.325, f32[4,512]{1,0:T(4,128)S(1)} %get-tuple-element.324, pred[2048]{0:T(1024)(128)(4,1)S(1)} %add_compare_fusion.2), kind=kLoop, calls=%fused_computation.5.clone.1 | loop fusion | flops 20969472 | bytes 16795648 | tf_op jit(solution)/shard_map/while/body/eval_jaxpr/reduce_sum | solution.py:29
  67.5 2.0 constant_dynamic-slice_fusion.12
  69.5 7.7 %fusion.86 = f32[64,4,8,128]{3,2,0,1:T(8,128)S(1)} fusion(bf16[1,2048,4,128]{3,2,1,0:T(4,128)(2,1)S(1)} %constant_dynamic-slice_fusion.12, f32[4,512,2048]{2,1,0:T(8,128)} %get-tuple-element.325, f32[4,512]{1,0:T(4,128)S(1)} %get-tuple-element.324, pred[2048]{0:T(1024)(128)(4,1)S(1)} %add_compare_fusion.2), kind=kOutput, calls=%fused_computation.11.clone.1 | convolution fusion | flops 1094713344 | bytes 19933184 | tf_op jit(solution)/shard_map/while/body/eval_jaxpr/kqp,pkd->kqd/dot_general | solution.py:30
  83.7 7.2 %fusion.81 = (f32[4,512]{1,0:T(4,128)S(1)}, f32[4,512,2048]{2,1,0:T(8,128)}) fusion(pred[2048]{0:T(1024)(128)(4,1)S(1)} %add_compare_fusion.2, bf16[1,2048,4,128]{3,2,1,0:T(4,128)(2,1)S(1)} %constant_dynamic-slice_fusion.9, bf16[4,64,32,128]{3,2,1,0:T(8,128)(2,1)S(1)} %copy-done, s32[]{:T(128)S(6)} %copy.150), kind=kOutput, calls=%fused_computation.3.clone.1 | convolution fusion | flops 1086322688 | bytes 19408900 | tf_op jit(solution)/shard_map/while/body/eval_jaxpr/kqd,pkd->kqp/dot_general | solution.py:23
  91.2 8.1 %fusion.82 = f32[4,512]{1,0:T(4,128)S(1)} fusion(f32[4,512,2048]{2,1,0:T(8,128)} %get-tuple-element.325, f32[4,512]{1,0:T(4,128)S(1)} %get-tuple-element.324, pred[2048]{0:T(1024)(128)(4,1)S(1)} %add_compare_fusion.2), kind=kLoop, calls=%fused_computation.5.clone.1 | loop fusion | flops 20969472 | bytes 16795648 | tf_op jit(solution)/shard_map/while/body/eval_jaxpr/reduce_sum | solution.py:29
  105.9 7.7 %fusion.86 = f32[64,4,8,128]{3,2,0,1:T(8,128)S(1)} fusion(bf16[1,2048,4,128]{3,2,1,0:T(4,128)(2,1)S(1)} %constant_dynamic-slice_fusion.12, f32[4,512,2048]{2,1,0:T(8,128)} %get-tuple-element.325, f32[4,512]{1,0:T(4,128)S(1)} %get-tuple-element.324, pred[2048]{0:T(1024)(128)(4,1)S(1)} %add_compare_fusion.2), kind=kOutput, calls=%fused_computation.11.clone.1 | convolution fusion | flops 1094713344 | bytes 19933184 | tf_op jit(solution)/shard_map/while/body/eval_jaxpr/kqp,pkd->kqd/dot_general | solution.py:30
  120.1 7.2 %fusion.81 = (f32[4,512]{1,0:T(4,128)S(1)}, f32[4,512,2048]{2,1,0:T(8,128)}) fusion(pred[2048]{0:T(1024)(128)(4,1)S(1)} %add_compare_fusion.2, bf16[1,2048,4,128]{3,2,1,0:T(4,128)(2,1)S(1)} %constant_dynamic-slice_fusion.9, bf16[4,64,32,128]{3,2,1,0:T(8,128)(2,1)S(1)} %copy-done, s32[]{:T(128)S(6)} %copy.150), kind=kOutput, calls=%fused_computation.3.clone.1 | convolution fusion | flops 1086322688 | bytes 19408900 | tf_op jit(solution)/shard_map/while/body/eval_jaxpr/kqd,pkd->kqp/dot_general | solution.py:23
  127.6 8.1 %fusion.82 = f32[4,512]{1,0:T(4,128)S(1)} fusion(f32[4,512,2048]{2,1,0:T(8,128)} %get-tuple-element.325, f32[4,512]{1,0:T(4,128)S(1)} %get-tuple-element.324, pred[2048]{0:T(1024)(128)(4,1)S(1)} %add_compare_fusion.2), kind=kLoop, calls=%fused_computation.5.clone.1 | loop fusion | flops 20969472 | bytes 16795648 | tf_op jit(solution)/shard_map/while/body/eval_jaxpr/reduce_sum | solution.py:29
  142.4 7.7 %fusion.86 = f32[64,4,8,128]{3,2,0,1:T(8,128)S(1)} fusion(bf16[1,2048,4,128]{3,2,1,0:T(4,128)(2,1)S(1)} %constant_dynamic-slice_fusion.12, f32[4,512,2048]{2,1,0:T(8,128)} %get-tuple-element.325, f32[4,512]{1,0:T(4,128)S(1)} %get-tuple-element.324, pred[2048]{0:T(1024)(128)(4,1)S(1)} %add_compare_fusion.2), kind=kOutput, calls=%fused_computation.11.clone.1 | convolution fusion | flops 1094713344 | bytes 19933184 | tf_op jit(solution)/shard_map/while/body/eval_jaxpr/kqp,pkd->kqd/dot_general | solution.py:30
  152.6 63.0 %pmax.7 = f32[256,32]{0,1:T(8,128)S(1)} all-reduce(f32[256,32]{0,1:T(8,128)S(1)} %reshape.71), channel_id=1, replica_groups=mesh['seq'=16,'head'=2] {'seq'}, use_global_device_ids=true, to_apply=%region_6.7 | all-reduce | flops 8192 | bytes 65536 | tf_op jit(solution)/shard_map/pmax | solution.py:86
  216.6 4.1 bitcast_multiply_fusion
  221.0 48.6 %reduce-scatter.10.cloned.1.call-done = f32[16,32]{1,0:T(8,128)} async-done(((f32[256,32]{1,0:T(8,128)}), f32[16,32]{1,0:T(8,128)}) %reduce-scatter.10.cloned.1.call-update) | async-done | bytes 2064
  270.5 74.7 %reduce-scatter.6.cloned.1.call-done = f32[16,32,128]{2,1,0:T(8,128)} async-done(((f32[256,32,128]{2,1,0:T(8,128)}), f32[16,32,128]{2,1,0:T(8,128)}) %reduce-scatter.6.cloned.1.call-update) | async-done | bytes 262160 | tf_op jit(solution)/shard_map/reduce_scatter | solution.py:90
  346.9 50.7 %all_to_all.5 = bf16[16,16,4096]{2,1,0:T(8,128)(2,1)S(1)} all-to-all(bf16[16,16,4096]{2,1,0:T(8,128)(2,1)S(1)} %stack.3), channel_id=1, replica_groups=mesh['seq'=16,'head'=2] {'seq'}, dimensions={0} | all-to-all | bytes 4194304 | tf_op jit(solution)/shard_map/all_to_all | solution.py:106
  397.6 2.0 fusion.35
  399.7 15.2 %reduce-scatter.8.cloned.1.call-done = f32[128,512]{1,0:T(8,128)} async-done(((f32[256,512]{1,0:T(8,128)}), f32[128,512]{1,0:T(8,128)}) %reduce-scatter.8.cloned.1.call-update) | async-done | bytes 262160 | tf_op jit(solution)/shard_map/reduce_scatter | solution.py:108
  (157 shorter events, 51.0 us)
Async XLA Ops:
  6.5 263.0 %reduce-scatter.10.cloned.1.call-start = ((), (), s32[]{:S(2)}) async-start(), calls=%async_computation.6 | async-start | bytes 139264
  6.6 4.2 copy-start
  43.0 4.2 copy-start
  79.5 4.2 copy-start
  116.0 4.2 copy-start
  216.5 128.7 %reduce-scatter.6.cloned.1.call-start = ((), (), s32[]{:S(2)}) async-start(), calls=%async_computation.4 | async-start | bytes 4456448 | tf_op jit(solution)/shard_map/reduce_scatter | solution.py:90
  220.8 194.1 %reduce-scatter.8.cloned.1.call-start = ((), (), s32[]{:S(2)}) async-start(), calls=%async_computation.5 | async-start | bytes 786432 | tf_op jit(solution)/shard_map/reduce_scatter | solution.py:108
  345.2 52.4 %copy-start.1 = (bf16[4096,512]{1,0:T(8,128)(2,1)S(1)}, bf16[4096,512]{1,0:T(8,128)(2,1)}, u32[]{:S(2)}) copy-start(bf16[4096,512]{1,0:T(8,128)(2,1)} %param.17) | copy-start | bytes 12582916
Sparse Core Ops, SparseCore 0:
  216.6 52.8 reduce-scatter.9
  273.4 71.7 reduce-scatter.5
  399.8 15.0 reduce-scatter.7
